TPU v7x, 32 devices: a whole 2x2x4 slice. The times are simulated.
32 devices in a mesh: scen: 8 (over z, x), row: 2 (over y), col: 2 (over core).
Axes of the slice: x: 2, y: 2, z: 4, core: 2. Of those that a mesh axis runs over, the one named last changes fastest.
Arguments:
- coupling: bfloat16 [24, 512, 3072], P('scen', None, ('row', 'col')), may hold values from -0.078125 to 0.078125
- factor_inv: bfloat16 [24, 512, 512], P('scen'), as said below
- block_mask: int32 [24, 4, 24], P('scen', None, ('row', 'col')), may hold values 0 or 1
Outputs:
- schur: float32 [2, 1536, 2, 2, 768], P('row', 'scen', None, 'col')
Inputs may be any that keep to these rules, and one draw needn't show every extreme that they name: factor_inv is lower triangular with a positive diagonal.
All inputs are finite; a program needn't handle non-finite values. No bound on the sum of `block_mask` on one device may be relied on, other than what follows from the above.
Results may differ from a plain program's by a relative error of at most 0.00064.
Values may be sent and summed in bfloat16 or wider, within the bound.
A program may use at most 64 MiB of HBM per device.

v0:
```python
import jax
import jax.numpy as jnp
from jax import lax
from jax.sharding import PartitionSpec as P

BLK = 128


def shards(coupling, factor_inv, block_mask):
    groups = coupling.shape[0]
    order = coupling.shape[1]
    width = coupling.shape[2]
    spread = jnp.broadcast_to(
        block_mask[:, :, None, :, None], (groups, order // BLK, BLK, width // BLK, BLK)
    )
    masked = coupling * spread.reshape(groups, order, width).astype(jnp.bfloat16)
    solved = jnp.einsum(
        "snk,skw->snw", factor_inv, masked, preferred_element_type=jnp.float32
    ).astype(jnp.bfloat16)
    left = lax.all_gather(solved, "col", axis=2, tiled=True)
    contract = (((0, 1), (0, 1)), ((), ()))
    tile_rows = left.shape[2]
    share = tile_rows // lax.axis_size("scen")
    tile = lax.dot_general(
        left,
        lax.all_gather(solved, "row", axis=2, tiled=True),
        contract,
        preferred_element_type=jnp.float32,
    )
    summed = lax.psum_scatter(tile, "scen", scatter_dimension=0, tiled=True)
    blocks = summed.shape[1] // width
    return summed.reshape(1, share, blocks, 1, width)


def solution(mesh):
    in_specs = (
        P("scen", None, ("row", "col")),
        P("scen", None, None),
        P("scen", None, ("row", "col")),
    )
    out_specs = P("row", "scen", None, "col", None)
    return jax.shard_map(shards, mesh=mesh, in_specs=in_specs, out_specs=out_specs, check_vma=False)
```

profile of v0, /device:TPU:0, one launch (start us, length us, event | category | flops | bytes accessed | tf_op | source)
XLA Modules:
  0.0 292.5 jit_solution(16594814116341144243)
XLA Ops:
  6.5 0.0 copy-start
  6.5 0.0 all-gather.3.cloned.1.call-start
  6.5 0.8 convert_element_type.13
  7.4 0.1 copy.7
  7.5 2.1 broadcast_in_dim.2
  9.6 5.1 %convert_element_type.14 = bf16[3,512,768]{1,2,0:T(8,128)(2,1)} reshape(bf16[3,4,128,6,128]{2,1,4,3,0:T(4,128)(2,1)} %broadcast_in_dim.2) | data formatting | bytes 4718592 | tf_op jit(solution)/shard_map/convert_element_type | solution.py:16
  14.7 4.3 %copy.8 = bf16[3,512,768]{1,2,0:T(8,128)(2,1)} copy(bf16[3,512,768]{2,1,0:T(8,128)(2,1)} %param.3) | data formatting | bytes 4718592 | tf_op args[0]
  19.0 0.0 copy-done
  19.0 5.2 %convert_bitcast_fusion = bf16[3,512,768]{1,2,0:T(8,128)(2,1)} fusion(bf16[3,512,512]{2,1,0:T(8,128)(2,1)S(1)} %copy-done, bf16[3,512,768]{1,2,0:T(8,128)(2,1)} %copy.8, bf16[3,512,768]{1,2,0:T(8,128)(2,1)} %convert_element_type.14), kind=kOutput, calls=%fused_computation.1 | convolution fusion | flops 1210318848 | bytes 8650752 | tf_op jit(solution)/shard_map/snk,skw->snw/dot_general | solution.py:17
  24.2 0.0 all-gather.3.cloned.1.call-update
  24.2 0.0 all-gather.5.cloned.1.call-start
  24.3 0.7 all-gather.5.cloned.1.call-update
  25.0 0.0 reduce-scatter.2.cloned.1.call-start
  25.0 16.5 %all-gather.3.cloned.1.call-done = bf16[3,512,1536]{1,2,0:T(8,128)(2,1)} async-done(((bf16[3,512,768]{1,2,0:T(8,128)(2,1)}), bf16[3,512,1536]{1,2,0:T(8,128)(2,1)}) %all-gather.3.cloned.1.call-update) | async-done | bytes 4718608 | tf_op jit(solution)/shard_map/all_gather | solution.py:20
  41.5 65.4 %all-gather.5.cloned.1.call-done = bf16[3,512,1536]{1,2,0:T(8,128)(2,1)} async-done(((bf16[3,512,768]{1,2,0:T(8,128)(2,1)}), bf16[3,512,1536]{1,2,0:T(8,128)(2,1)}) %all-gather.5.cloned.1.call-update) | async-done | bytes 4718608 | tf_op jit(solution)/shard_map/all_gather | solution.py:26
  106.9 13.2 %convolution_bitcast_fusion = f32[1536,1536]{1,0:T(8,128)} fusion(bf16[3,512,1536]{1,2,0:T(8,128)(2,1)} %all-gather.3.cloned.1.call-done, bf16[3,512,1536]{1,2,0:T(8,128)(2,1)} %all-gather.5.cloned.1.call-done), kind=kOutput, calls=%fused_computation | convolution fusion | flops 7247757312 | bytes 18874368 | tf_op jit(solution)/shard_map/dot_general | solution.py:24
  120.2 0.0 reduce-scatter.2.cloned.1.call-update
  120.2 162.3 %reduce-scatter.2.cloned.1.call-done = f32[192,1536]{1,0:T(8,128)} async-done(((f32[1536,1536]{1,0:T(8,128)}), f32[192,1536]{1,0:T(8,128)}) %reduce-scatter.2.cloned.1.call-update) | async-done | bytes 1179664 | tf_op jit(solution)/shard_map/reduce_scatter | solution.py:30
  282.4 3.5 %reshape.8 = f32[1,192,2,1,768]{4,3,2,1,0:T(1,128)} reshape(f32[192,1536]{1,0:T(8,128)} %reduce-scatter.2.cloned.1.call-done) | data formatting | bytes 2359296 | tf_op jit(solution)/shard_map/reshape | solution.py:32
Async XLA Ops:
  6.5 12.4 %copy-start = (bf16[3,512,512]{2,1,0:T(8,128)(2,1)S(1)}, bf16[3,512,512]{2,1,0:T(8,128)(2,1)}, u32[]{:S(2)}) copy-start(bf16[3,512,512]{2,1,0:T(8,128)(2,1)} %param.4) | copy-start | bytes 4718596
  6.5 35.0 %all-gather.3.cloned.1.call-start = ((), (), s32[]{:S(2)}) async-start(), calls=%async_computation.1 | async-start | bytes 7077888 | tf_op jit(solution)/shard_map/all_gather | solution.py:20
  24.2 82.7 %all-gather.5.cloned.1.call-start = ((), (), s32[]{:S(2)}) async-start(), calls=%async_computation.2 | async-start | bytes 7077888 | tf_op jit(solution)/shard_map/all_gather | solution.py:26
  25.0 257.5 %reduce-scatter.2.cloned.1.call-start = ((), (), s32[]{:S(2)}) async-start(), calls=%async_computation.3 | async-start | bytes 10616832 | tf_op jit(solution)/shard_map/reduce_scatter | solution.py:30
Sparse Core Ops, SparseCore 0:
  24.3 17.1 all-gather.2
  43.1 63.7 all-gather.4
  120.3 162.0 reduce-scatter.1
where the time goes:
time: 293 us
  waiting for transfers between devices  245 us (84%)
  matrix products  18.4 us (6%)
  local copies, waits for them, and re-layouts  15.2 us (5%)
  between operations  13.1 us (4%)
    reduce_scatter x1, waiting for transfers between devices, shards(): summed = lax.psum_scatter(tile, 'scen', scatter_dimension=0, tiled=True)  162 us
    all_gather x1, waiting for transfers between devices, shards(): lax.all_gather(solved, 'row', axis=2, tiled=True)  65.4 us
    all_gather x1, waiting for transfers between devices, shards(): left = lax.all_gather(solved, 'col', axis=2, tiled=True)  16.5 us
    dot_general x1, matrix products, shards(): lax.dot_general(left, lax.all_gather(solved, 'row', axis=2, tiled=True),...  13.2 us
  transfers between devices with their start and end apart: 3, of which 3 were waited for; matrix products, arithmetic and copies ran while one was open for 0% of the time, Pallas kernels for 0%

commit v1 on v0

v1 whole, which is shorter than its diff:
```python
import functools

import jax
import jax.numpy as jnp
from jax import lax
from jax.experimental import pallas as pl
from jax.experimental.pallas import tpu as pltpu
from jax.sharding import PartitionSpec as P

BLK = 128
PIECE = 256
HALF = PIECE // 2
HEAD = 16
LINK = jnp.int16
FINE = 64.0
TOP = 14.9
MESH = pl.DeviceIdType.MESH
NT = (((1,), (1,)), ((), ()))


def encode(value):
    most = jnp.maximum(jnp.max(jnp.abs(value), axis=0, keepdims=True), 1e-30)
    power = jnp.ceil(jnp.log2(most) * FINE)
    scaled = jnp.round(value * jnp.exp2(TOP - power / FINE))
    head = jnp.broadcast_to(power, (HEAD, value.shape[1]))
    return head.astype(jnp.int32).astype(LINK), scaled.astype(jnp.int32).astype(LINK)


def decode(head, scaled):
    power = head.astype(jnp.int32).astype(jnp.float32)[0:1, :]
    return scaled.astype(jnp.int32).astype(jnp.float32) * jnp.exp2(power / FINE - TOP)


def kernel(n, n_row, coupling, factor, mask, out, left, right, partial, held, sent,
           col_send, col_recv, row_send, row_recv, ring_send, ring_recv):
    groups, order, width = coupling.shape
    share = out.shape[0]
    pieces = width // PIECE
    scen, row, col = lax.axis_index("scen"), lax.axis_index("row"), lax.axis_index("col")

    half = n // 2
    side, depth = lax.rem(scen, 2), scen // 2
    place = jnp.where(side == 0, depth, n - 1 - depth)

    def at(position):
        position = lax.rem(position + 2 * n, n)
        return jnp.where(position < half, 2 * position, 2 * (n - 1 - position) + 1)

    around = (at(place + 1), at(place - 1))
    partners = [lax.rem(row + n_row - d, n_row) for d in range(1, n_row)]
    barrier = pltpu.get_barrier_semaphore()
    for target in around:
        pl.semaphore_signal(barrier, inc=1, device_id=(target, row, col), device_id_type=MESH)
    for target in partners:
        pl.semaphore_signal(barrier, inc=1, device_id=(scen, target, col), device_id_type=MESH)
    pl.semaphore_signal(barrier, inc=1, device_id=(scen, row, 1 - col), device_id_type=MESH)

    mine = pl.ds(pl.multiple_of(col * width, width), width)
    col_copies, row_copies = [], []
    for g in range(groups):
        rows = []
        for i in range(order // BLK):
            rows.append(jnp.concatenate([
                coupling[g, i * BLK:(i + 1) * BLK, j * BLK:(j + 1) * BLK]
                * mask[g, i, j].astype(jnp.float32).astype(jnp.bfloat16)
                for j in range(width // BLK)], axis=1))
        masked = jnp.concatenate(rows, axis=0)
        solved = jnp.dot(factor[g], masked, preferred_element_type=jnp.float32)
        left[g, mine, :] = solved.T.astype(jnp.bfloat16)
        if g == 0:
            pl.semaphore_wait(barrier, 2 + n_row)
        copy = pltpu.make_async_remote_copy(
            src_ref=left.at[g, mine], dst_ref=left.at[g, mine],
            send_sem=col_send.at[g], recv_sem=col_recv.at[g],
            device_id=(scen, row, 1 - col), device_id_type=MESH)
        copy.start()
        col_copies.append(copy)
    for k in range(pieces):
        for d in range(1, n_row):
            copy = pltpu.make_async_remote_copy(
                src_ref=left.at[:, pl.ds(pl.multiple_of(col * width + k * PIECE, PIECE), PIECE)],
                dst_ref=right.at[d - 1, :, pl.ds(k * PIECE, PIECE)],
                send_sem=row_send.at[d - 1, k], recv_sem=row_recv.at[d - 1, k],
                device_id=(scen, partners[d - 1], col), device_id_type=MESH)
            copy.start()
            row_copies.append(copy)

    ring_copies = {}

    def multiply(phase):
        d, k = phase // pieces, phase % pieces
        if d == 0:
            def block(g):
                return left[g, pl.ds(pl.multiple_of(col * width + k * PIECE, PIECE), PIECE), :]
        else:
            row_copies[k * (n_row - 1) + d - 1].wait_recv()

            def block(g):
                return right[d - 1, g, k * PIECE:(k + 1) * PIECE, :]

        @pl.loop(0, 2)
        def _(b):
            rows = pl.ds(pl.multiple_of(b * width, width), width)
            total = lax.dot_general(left[0, rows, :], block(0), NT, preferred_element_type=jnp.float32)
            for g in range(1, groups):
                total += lax.dot_general(left[g, rows, :], block(g), NT, preferred_element_type=jnp.float32)
            partial[phase, pl.ds(b * half, half)] = total.reshape(half, share, PIECE)

    def hop(phase, way, step):
        lanes = slice(way * HALF, (way + 1) * HALF)
        chunk = at(place - 1 - step) if way == 0 else at(place + 1 + step)
        value = partial[phase, chunk, :, lanes]
        if step:
            ring_copies[phase, way, step - 1].wait_recv()
            value += decode(held[phase, way, step - 1, 0:HEAD, :], held[phase, way, step - 1, HEAD:, :])
        if step == n - 1:
            d, k = phase // pieces, phase % pieces
            start = lax.rem(row + d, n_row) * width + k * PIECE + way * HALF
            out[:, pl.ds(pl.multiple_of(start, HALF), HALF)] = value
            return
        head, scaled = encode(value)
        sent[phase, way, step, 0:HEAD, :] = head
        sent[phase, way, step, HEAD:, :] = scaled
        copy = pltpu.make_async_remote_copy(
            src_ref=sent.at[phase, way, step], dst_ref=held.at[phase, way, step],
            send_sem=ring_send.at[phase, way, step], recv_sem=ring_recv.at[phase, way, step],
            device_id=(around[way], row, col), device_id_type=MESH)
        copy.start()
        ring_copies[phase, way, step] = copy

    for copy in col_copies:
        copy.wait_recv()
    starts = [0] * pieces + [n - 2 + 5 * (i // (n_row - 1)) for i in range(pieces * (n_row - 1))]
    order_of = list(range(pieces)) + [d * pieces + k for k in range(pieces) for d in range(1, n_row)]
    for tick in range(max(starts) + n):
        for phase, start in zip(order_of, starts):
            step = tick - start
            if step == 0:
                multiply(phase)
            if 0 <= step < n:
                hop(phase, 0, step)
                hop(phase, 1, step)
    for copy in col_copies + row_copies + list(ring_copies.values()):
        copy.wait_send()


def fused(n, n_row, coupling, factor_inv, block_mask):
    groups, order, width = coupling.shape
    rows = 2 * width
    share = rows // n
    phases = n_row * width // PIECE
    message = (phases, 2, n - 1, HEAD + share, HALF)
    vmem = pl.BlockSpec(memory_space=pltpu.VMEM)
    tile = pl.pallas_call(
        functools.partial(kernel, n, n_row),
        out_shape=jax.ShapeDtypeStruct((share, n_row * width), jnp.float32),
        in_specs=[vmem, vmem, pl.BlockSpec(memory_space=pltpu.SMEM)],
        out_specs=vmem,
        scratch_shapes=[
            pltpu.VMEM((groups, rows, order), jnp.bfloat16),
            pltpu.VMEM((n_row - 1, groups, width, order), jnp.bfloat16),
            pltpu.VMEM((phases, n, share, PIECE), jnp.float32),
            pltpu.VMEM(message, LINK),
            pltpu.VMEM(message, LINK),
            pltpu.SemaphoreType.DMA((groups,)),
            pltpu.SemaphoreType.DMA((groups,)),
            pltpu.SemaphoreType.DMA((n_row - 1, width // PIECE)),
            pltpu.SemaphoreType.DMA((n_row - 1, width // PIECE)),
            pltpu.SemaphoreType.DMA(message[:3]),
            pltpu.SemaphoreType.DMA(message[:3]),
        ],
        compiler_params=pltpu.CompilerParams(
            collective_id=0, has_side_effects=True, vmem_limit_bytes=60 * 1024 * 1024),
    )(coupling, factor_inv, block_mask)
    return tile.reshape(1, share, n_row, 1, width)


def plain(coupling, factor_inv, block_mask):
    groups, order, width = coupling.shape
    spread = jnp.broadcast_to(
        block_mask[:, :, None, :, None], (groups, order // BLK, BLK, width // BLK, BLK)
    )
    masked = coupling * spread.reshape(groups, order, width).astype(jnp.bfloat16)
    solved = jnp.einsum(
        "snk,skw->snw", factor_inv, masked, preferred_element_type=jnp.float32
    ).astype(jnp.bfloat16)
    left = lax.all_gather(solved, "col", axis=2, tiled=True)
    share = left.shape[2] // lax.axis_size("scen")
    tile = lax.dot_general(
        left,
        lax.all_gather(solved, "row", axis=2, tiled=True),
        (((0, 1), (0, 1)), ((), ())),
        preferred_element_type=jnp.float32,
    )
    summed = lax.psum_scatter(tile, "scen", scatter_dimension=0, tiled=True)
    return summed.reshape(1, share, summed.shape[1] // width, 1, width)


def solution(mesh):
    n, n_row = mesh.shape["scen"], mesh.shape["row"]

    def shards(coupling, factor_inv, block_mask):
        width = coupling.shape[2]
        share = 2 * width // n
        if share % 16 == 0 and width % PIECE == 0 and n % 2 == 0 and n > 2 and n_row > 1:
            return fused(n, n_row, coupling, factor_inv, block_mask)
        return plain(coupling, factor_inv, block_mask)

    in_specs = (
        P("scen", None, ("row", "col")),
        P("scen", None, None),
        P("scen", None, ("row", "col")),
    )
    out_specs = P("row", "scen", None, "col", None)
    return jax.shard_map(shards, mesh=mesh, in_specs=in_specs, out_specs=out_specs, check_vma=False)
```

time: 293 us -> 105 us (0.36)
  waiting for transfers between devices: 245 us -> 0 us
  Pallas kernels: 0 us -> 102 us
  matrix products: 18.4 us -> 0 us
  between operations: 13.1 us -> 0.01 us
  local copies, waits for them, and re-layouts: 15.2 us -> 3.55 us
    reduce_scatter x1 -> x0, waiting for transfers between devices: 162 us -> none  [shards(): summed = lax.psum_scatter(tile, 'scen', scatter_dimension=0, tiled=True)]
    pallas_call x0 -> x1, Pallas kernels: none -> 102 us  [fused(): pl.pallas_call(functools.partial(kernel, n, n_row), out_shape=jax.ShapeDt...]
    all_gather x2 -> x0, waiting for transfers between devices: 81.9 us -> none  [the longest x1 65.4 us: shards(): lax.all_gather(solved, 'row', axis=2, tiled=True)]
    dot_general x2 -> x0, matrix products: 18.4 us -> none  [the longest x1 13.2 us: shards(): lax.dot_general(left, lax.all_gather(solved, 'row', axis=2, tiled=True),...]
    convert_element_type x2 -> x0, local copies, waits for them, and re-layouts: 5.26 us -> none  [shards(): spread.reshape(groups, order, width).astype(jnp.bfloat16)]
    unnamed x3 -> x0, local copies, waits for them, and re-layouts: 4.29 us -> none
  transfers between devices with their start and end apart: 3 -> 0, of which waited for: 3 -> 0; matrix products, arithmetic and copies ran while one was open for 0% -> 0% of each run, Pallas kernels for 0% -> 0%
where the time goes in v1:
time: 105 us
  Pallas kernels  102 us (97%)
  local copies, waits for them, and re-layouts  3.55 us (3%)
    pallas_call x1, Pallas kernels, fused(): pl.pallas_call(functools.partial(kernel, n, n_row), out_shape=jax.ShapeDt...  102 us
    reshape x1, local copies, waits for them, and re-layouts, fused(): return tile.reshape(1, share, n_row, 1, width)  3.55 us

profile of v1, /device:TPU:0, one launch (start us, length us, event | category | flops | bytes accessed | tf_op | source)
XLA Modules:
  0.0 105.3 jit_solution(7616868812881605897)
XLA Ops:
  0.0 101.7 %shard_map.37 = f32[192,1536]{1,0:T(8,128)} custom-call(bf16[3,512,768]{2,1,0:T(8,128)(2,1)} %coupling.1, bf16[3,512,512]{2,1,0:T(8,128)(2,1)} %factor.1, s32[3,4,6]{2,1,0:T(4,128)} %mask.1), custom_call_target="tpu_custom_call" | custom-call | tf_op jit(solution)/shard_map/pallas_call | solution.py:154
  101.7 3.6 %reshape.4 = f32[1,192,2,1,768]{4,3,2,1,0:T(1,128)} reshape(f32[192,1536]{1,0:T(8,128)} %shard_map.37) | data formatting | bytes 2359296 | tf_op jit(solution)/shard_map/reshape | solution.py:175

commit v2 on v1

--- a/solution.py
+++ b/solution.py
@@ -14,6 +14,7 @@
 LINK = jnp.int16
 FINE = 64.0
 TOP = 14.9
+STARTS = (4, 7, 9, 10)
 MESH = pl.DeviceIdType.MESH
 NT = (((1,), (1,)), ((), ()))
 
@@ -31,11 +32,13 @@
     return scaled.astype(jnp.int32).astype(jnp.float32) * jnp.exp2(power / FINE - TOP)
 
 
-def kernel(n, n_row, coupling, factor, mask, out, left, right, partial, held, sent,
-           col_send, col_recv, row_send, row_recv, ring_send, ring_recv):
+def kernel(n, n_row, coupling, factor, mask, out, left, right,
+           col_send, col_recv, row_send, row_recv, ring_send, ring_recv, *buffers):
     groups, order, width = coupling.shape
     share = out.shape[0]
-    pieces = width // PIECE
+    phases = phases_of(n_row, width)
+    partial, held, sent = [buffers[i * len(phases):(i + 1) * len(phases)] for i in range(3)]
+    late = sorted({phase[1:3] for phase in phases if phase[0]})
     scen, row, col = lax.axis_index("scen"), lax.axis_index("row"), lax.axis_index("col")
 
     half = n // 2
@@ -56,7 +59,19 @@
     pl.semaphore_signal(barrier, inc=1, device_id=(scen, row, 1 - col), device_id_type=MESH)
 
     mine = pl.ds(pl.multiple_of(col * width, width), width)
-    col_copies, row_copies = [], []
+    col_copies, row_copies = [], {}
+
+    def row_send_piece(g, k):
+        base, count = late[k]
+        for d in range(1, n_row):
+            copy = pltpu.make_async_remote_copy(
+                src_ref=left.at[g, pl.ds(pl.multiple_of(col * width + base, HALF), count)],
+                dst_ref=right.at[d - 1, g, pl.ds(base, count)],
+                send_sem=row_send.at[d - 1, k, g], recv_sem=row_recv.at[d - 1, k, g],
+                device_id=(scen, partners[d - 1], col), device_id_type=MESH)
+            copy.start()
+            row_copies[d, base, g] = copy
+
     for g in range(groups):
         rows = []
         for i in range(order // BLK):
@@ -75,81 +90,96 @@
             device_id=(scen, row, 1 - col), device_id_type=MESH)
         copy.start()
         col_copies.append(copy)
-    for k in range(pieces):
-        for d in range(1, n_row):
-            copy = pltpu.make_async_remote_copy(
-                src_ref=left.at[:, pl.ds(pl.multiple_of(col * width + k * PIECE, PIECE), PIECE)],
-                dst_ref=right.at[d - 1, :, pl.ds(k * PIECE, PIECE)],
-                send_sem=row_send.at[d - 1, k], recv_sem=row_recv.at[d - 1, k],
-                device_id=(scen, partners[d - 1], col), device_id_type=MESH)
-            copy.start()
-            row_copies.append(copy)
+        row_send_piece(g, 0)
+    for k in range(1, len(late)):
+        for g in range(groups):
+            row_send_piece(g, k)
 
     ring_copies = {}
 
-    def multiply(phase):
-        d, k = phase // pieces, phase % pieces
-        if d == 0:
-            def block(g):
-                return left[g, pl.ds(pl.multiple_of(col * width + k * PIECE, PIECE), PIECE), :]
+    def multiply(phase, b):
+        d, base, count, _ = phases[phase]
+
+        def block(g):
+            if d:
+                return right[d - 1, g, base:base + count, :]
+            return left[g, pl.ds(pl.multiple_of(col * width + base, HALF), count), :]
+
+        rows = pl.ds(pl.multiple_of(b * width, width), width)
+        total = lax.dot_general(left[0, rows, :], block(0), NT, preferred_element_type=jnp.float32)
+        for g in range(1, groups):
+            total += lax.dot_general(left[g, rows, :], block(g), NT, preferred_element_type=jnp.float32)
+        partial[phase][pl.ds(b * half, half)] = total.reshape(half, share, count)
+
+    def hop(phase, way, step):
+        d, base, count, by_rows = phases[phase]
+        if by_rows:
+            rows, lanes = slice(way * share // 2, (way + 1) * share // 2), slice(0, count)
         else:
-            row_copies[k * (n_row - 1) + d - 1].wait_recv()
-
-            def block(g):
-                return right[d - 1, g, k * PIECE:(k + 1) * PIECE, :]
-
-        @pl.loop(0, 2)
-        def _(b):
-            rows = pl.ds(pl.multiple_of(b * width, width), width)
-            total = lax.dot_general(left[0, rows, :], block(0), NT, preferred_element_type=jnp.float32)
-            for g in range(1, groups):
-                total += lax.dot_general(left[g, rows, :], block(g), NT, preferred_element_type=jnp.float32)
-            partial[phase, pl.ds(b * half, half)] = total.reshape(half, share, PIECE)
-
-    def hop(phase, way, step):
-        lanes = slice(way * HALF, (way + 1) * HALF)
+            rows, lanes = slice(0, share), slice(way * count // 2, (way + 1) * count // 2)
         chunk = at(place - 1 - step) if way == 0 else at(place + 1 + step)
-        value = partial[phase, chunk, :, lanes]
+        value = partial[phase][chunk, rows, lanes]
         if step:
             ring_copies[phase, way, step - 1].wait_recv()
-            value += decode(held[phase, way, step - 1, 0:HEAD, :], held[phase, way, step - 1, HEAD:, :])
+            came = held[phase]
+            value += decode(came[way, step - 1, 0:HEAD, :], came[way, step - 1, HEAD:, :])
         if step == n - 1:
-            d, k = phase // pieces, phase % pieces
-            start = lax.rem(row + d, n_row) * width + k * PIECE + way * HALF
-            out[:, pl.ds(pl.multiple_of(start, HALF), HALF)] = value
+            start = lax.rem(row + d, n_row) * width + base + lanes.start
+            out[rows, pl.ds(pl.multiple_of(start, HALF), lanes.stop - lanes.start)] = value
             return
         head, scaled = encode(value)
-        sent[phase, way, step, 0:HEAD, :] = head
-        sent[phase, way, step, HEAD:, :] = scaled
+        sent[phase][way, step, 0:HEAD, :] = head
+        sent[phase][way, step, HEAD:, :] = scaled
         copy = pltpu.make_async_remote_copy(
-            src_ref=sent.at[phase, way, step], dst_ref=held.at[phase, way, step],
+            src_ref=sent[phase].at[way, step], dst_ref=held[phase].at[way, step],
             send_sem=ring_send.at[phase, way, step], recv_sem=ring_recv.at[phase, way, step],
             device_id=(around[way], row, col), device_id_type=MESH)
         copy.start()
         ring_copies[phase, way, step] = copy
 
+    early = [phase for phase in range(len(phases)) if phases[phase][0] == 0]
+    for phase in early:
+        multiply(phase, col)
     for copy in col_copies:
         copy.wait_recv()
-    starts = [0] * pieces + [n - 2 + 5 * (i // (n_row - 1)) for i in range(pieces * (n_row - 1))]
-    order_of = list(range(pieces)) + [d * pieces + k for k in range(pieces) for d in range(1, n_row)]
+    starts = [0 if phase in early else STARTS[min(late.index(phases[phase][1:3]), len(STARTS) - 1)]
+              for phase in range(len(phases))]
     for tick in range(max(starts) + n):
-        for phase, start in zip(order_of, starts):
+        for phase, start in enumerate(starts):
             step = tick - start
-            if step == 0:
-                multiply(phase)
+            if step == 0 and phase in early:
+                multiply(phase, 1 - col)
+            elif step == 0:
+                d, base = phases[phase][:2]
+                for g in range(groups):
+                    row_copies[d, base, g].wait_recv()
+
+                @pl.loop(0, 2)
+                def _(b):
+                    multiply(phase, b)
             if 0 <= step < n:
                 hop(phase, 0, step)
                 hop(phase, 1, step)
-    for copy in col_copies + row_copies + list(ring_copies.values()):
+    for copy in col_copies + list(row_copies.values()) + list(ring_copies.values()):
         copy.wait_send()
+
+
+def phases_of(n_row, width):
+    early = [(0, base, PIECE, False) for base in range(0, width, PIECE)]
+    late = [(base, PIECE, False) for base in range(0, width - PIECE, PIECE)]
+    late += [(base, HALF, True) for base in (width - PIECE, width - HALF)]
+    return early + [(d, *piece) for piece in late for d in range(1, n_row)]
 
 
 def fused(n, n_row, coupling, factor_inv, block_mask):
     groups, order, width = coupling.shape
     rows = 2 * width
     share = rows // n
-    phases = n_row * width // PIECE
-    message = (phases, 2, n - 1, HEAD + share, HALF)
+    phases = phases_of(n_row, width)
+    late = len(phases) - width // PIECE
+    shapes = [(2, n - 1, HEAD + (share // 2 if by_rows else share), HALF) for _, _, _, by_rows in phases]
+    partials = [pltpu.VMEM((n, share, count), jnp.float32) for _, _, count, _ in phases]
+    messages = [pltpu.VMEM(shape, LINK) for shape in shapes]
     vmem = pl.BlockSpec(memory_space=pltpu.VMEM)
     tile = pl.pallas_call(
         functools.partial(kernel, n, n_row),
@@ -159,15 +189,13 @@
         scratch_shapes=[
             pltpu.VMEM((groups, rows, order), jnp.bfloat16),
             pltpu.VMEM((n_row - 1, groups, width, order), jnp.bfloat16),
-            pltpu.VMEM((phases, n, share, PIECE), jnp.float32),
-            pltpu.VMEM(message, LINK),
-            pltpu.VMEM(message, LINK),
             pltpu.SemaphoreType.DMA((groups,)),
             pltpu.SemaphoreType.DMA((groups,)),
-            pltpu.SemaphoreType.DMA((n_row - 1, width // PIECE)),
-            pltpu.SemaphoreType.DMA((n_row - 1, width // PIECE)),
-            pltpu.SemaphoreType.DMA(message[:3]),
-            pltpu.SemaphoreType.DMA(message[:3]),
+            pltpu.SemaphoreType.DMA((n_row - 1, late, groups)),
+            pltpu.SemaphoreType.DMA((n_row - 1, late, groups)),
+            pltpu.SemaphoreType.DMA((len(phases), 2, n - 1)),
+            pltpu.SemaphoreType.DMA((len(phases), 2, n - 1)),
+            *partials, *messages, *messages,
         ],
         compiler_params=pltpu.CompilerParams(
             collective_id=0, has_side_effects=True, vmem_limit_bytes=60 * 1024 * 1024),
@@ -202,7 +230,7 @@
     def shards(coupling, factor_inv, block_mask):
         width = coupling.shape[2]
         share = 2 * width // n
-        if share % 16 == 0 and width % PIECE == 0 and n % 2 == 0 and n > 2 and n_row > 1:
+        if share % 32 == 0 and width % PIECE == 0 and n % 2 == 0 and n > 2 and n_row > 1:
             return fused(n, n_row, coupling, factor_inv, block_mask)
         return plain(coupling, factor_inv, block_mask)
 

time: 105 us -> 88.6 us (0.84)
  Pallas kernels: 102 us -> 84.9 us
    pallas_call x1, Pallas kernels: 102 us -> 84.9 us  [fused(): pl.pallas_call(functools.partial(kernel, n, n_row), out_shape=jax.ShapeDt...]
where the time goes in v2:
time: 88.6 us; the launch traced here: 88.5 us
  Pallas kernels  84.9 us (96%)
  local copies, waits for them, and re-layouts  3.55 us (4%)
    pallas_call x1, Pallas kernels, fused(): pl.pallas_call(functools.partial(kernel, n, n_row), out_shape=jax.ShapeDt...  84.9 us
    reshape x1, local copies, waits for them, and re-layouts, fused(): return tile.reshape(1, share, n_row, 1, width)  3.55 us

profile of v2, /device:TPU:0, one launch (start us, length us, event | category | flops | bytes accessed | tf_op | source)
XLA Modules:
  0.0 88.5 jit_solution(14246511203167414448)
XLA Ops:
  0.0 84.9 %shard_map.37 = f32[192,1536]{1,0:T(8,128)} custom-call(bf16[3,512,768]{2,1,0:T(8,128)(2,1)} %coupling.1, bf16[3,512,512]{2,1,0:T(8,128)(2,1)} %factor.1, s32[3,4,6]{2,1,0:T(4,128)} %mask.1), custom_call_target="tpu_custom_call" | custom-call | tf_op jit(solution)/shard_map/pallas_call | solution.py:184
  84.9 3.6 %reshape.4 = f32[1,192,2,1,768]{4,3,2,1,0:T(1,128)} reshape(f32[192,1536]{1,0:T(8,128)} %shard_map.37) | data formatting | bytes 2359296 | tf_op jit(solution)/shard_map/reshape | solution.py:203
